TPU v7x, 512 devices: a whole 4x4x16 slice. The times are simulated.
512 devices in a mesh: dp: 32 (over z, core), expert: 16 (over x, y).
Axes of the slice: x: 4, y: 4, z: 16, core: 2. Of those that a mesh axis runs over, the one named last changes fastest.
Arguments:
- tokens: bfloat16 [5120, 4096], P('expert', 'dp'), may hold values from -6 to 6
- out_grad: bfloat16 [5120, 4096], P('expert', 'dp'), may hold values from -0.29882812 to 0.29882812
- slot_tokens: int32 [4, 160], replicated, may hold values from 0 to 5119, as said below
- slot_gate: float32 [4, 160], replicated, may hold values from 0.1 to 1
- w_gate: bfloat16 [16, 4096, 2048], P('expert', 'dp'), may hold values from -0.09375 to 0.09375
- w_up: bfloat16 [16, 4096, 2048], P('expert', 'dp'), may hold values from -0.09375 to 0.09375
- w_down: bfloat16 [16, 2048, 4096], P('expert', None, 'dp'), may hold values from -0.0625 to 0.0625
Outputs:
- grad_tokens: bfloat16 [5120, 4096], P('expert', 'dp')
- grad_w_gate: bfloat16 [16, 4096, 2048], P('expert', 'dp')
- grad_w_up: bfloat16 [16, 4096, 2048], P('expert', 'dp')
- grad_w_down: bfloat16 [16, 2048, 4096], P('expert', None, 'dp')
- grad_gates: float32 [16, 40], P('expert')
Inputs may be any that keep to these rules, and one draw needn't show every extreme that they name: `slot_tokens`: row e lists 160 distinct token numbers, ordered by their owner t // 320 ascending. At most 20 of a row come from the 320 tokens of one owner, and in every row exactly 20 come from one owner.
All inputs are finite; a program needn't handle non-finite values.
Results may differ from a plain program's by a relative error of at most 0.0057.
Values may be sent and summed in bfloat16 or wider, within the bound.
No kernel may reach another device: no remote copies, remote signals or barrier semaphores. Data moves between devices by JAX's collectives and lax.ppermute only.
A program may use at most 64 MiB of HBM per device.

v0:
```python
import jax
import jax.numpy as jnp
from jax import lax
from jax.sharding import PartitionSpec as P

GROUP = 4


def partner(value, axis, distance):
    mask = 2**distance
    pairs = [(source, source ^ mask) for source in range(lax.axis_size(axis))]
    return lax.ppermute(value, axis, pairs)


def contract_rows(left, right):
    return lax.dot_general(
        left, right, (((0,), (0,)), ((), ())), preferred_element_type=jnp.float32
    )


def contract_cols(left, right):
    return lax.dot_general(
        left, right, (((1,), (1,)), ((), ())), preferred_element_type=jnp.float32
    )


def slot_ranking(owners, owner_count):
    owner_range = jnp.arange(owner_count, dtype=jnp.int32)
    onehot = (owners[:, :, None] == owner_range[None, None, :]).astype(jnp.int32)
    before = jnp.cumsum(onehot, axis=1) - onehot
    return jnp.sum(before * onehot, axis=2)


def gated_grads(upstream, pre_gate, pre_up, sigmoid_gate):
    gate_side = (upstream * pre_up * sigmoid_gate * (1.0 + pre_gate * (1.0 - sigmoid_gate))).astype(
        jnp.bfloat16
    )
    up_side = (upstream * pre_gate * sigmoid_gate).astype(jnp.bfloat16)
    return (gate_side, up_side)


def per_device(tokens, out_grad, slot_tokens, slot_gate, w_gate, w_up, w_down):
    owner_count = lax.axis_size("expert")
    position = lax.axis_index("expert")
    token_rows = tokens.shape[0]
    feature_cols = tokens.shape[1]
    flight_count, capacity = slot_tokens.shape
    bucket_size = GROUP * max(1, capacity // (2 * owner_count))
    owners = slot_tokens // token_rows
    slot_rank = slot_ranking(owners, owner_count)
    is_mine = owners == position
    local_index = slot_tokens - position * token_rows
    expert_rows = jnp.broadcast_to(
        jnp.arange(flight_count, dtype=jnp.int32)[:, None], (flight_count, capacity)
    )
    column_index = jnp.where(is_mine, slot_rank, bucket_size)
    send_table = (
        jnp.zeros((flight_count, bucket_size + 1), jnp.int32)
        .at[expert_rows, column_index]
        .set(local_index)[:, :bucket_size]
    )
    filled = (
        jnp.zeros((flight_count, bucket_size + 1), jnp.int32)
        .at[expert_rows, column_index]
        .set(1)[:, :bucket_size]
    )
    send_index = jnp.repeat(send_table, GROUP, axis=0)
    send_valid = jnp.repeat(filled, GROUP, axis=0) > 0
    input_send = jnp.where(send_valid[:, :, None], tokens[send_index], jnp.zeros((), jnp.bfloat16))
    grad_send = jnp.where(send_valid[:, :, None], out_grad[send_index], jnp.zeros((), jnp.bfloat16))
    input_recv, grad_recv = (
        lax.all_to_all(input_send, "expert", split_axis=0, concat_axis=0, tiled=True),
        lax.all_to_all(grad_send, "expert", split_axis=0, concat_axis=0, tiled=True),
    )
    expert_here = position // GROUP
    quarter = position % GROUP
    owner_here = lax.dynamic_index_in_dim(owners, expert_here, 0, keepdims=False)
    rank_here = lax.dynamic_index_in_dim(slot_rank, expert_here, 0, keepdims=False)
    bucket_flat = owner_here * bucket_size + rank_here
    slot_inputs = input_recv.reshape(owner_count * bucket_size, feature_cols)[bucket_flat]
    slot_grads = grad_recv.reshape(owner_count * bucket_size, feature_cols)[bucket_flat]
    gates_here = lax.dynamic_index_in_dim(slot_gate, expert_here, 0, keepdims=False)
    gate_weight = w_gate[0]
    up_weight = w_up[0]
    down_weight = w_down[0]
    part_gate = jnp.dot(slot_inputs, gate_weight, preferred_element_type=jnp.float32)
    part_up = jnp.dot(slot_inputs, up_weight, preferred_element_type=jnp.float32)
    pre_gate, pre_up = lax.psum((part_gate, part_up), "dp")
    sigmoid_gate = jax.nn.sigmoid(pre_gate)
    hidden = (pre_gate * sigmoid_gate * pre_up).astype(jnp.bfloat16)
    local_out = jnp.dot(hidden, down_weight, preferred_element_type=jnp.float32)
    gate_part = jnp.sum(slot_grads.astype(jnp.float32) * local_out, axis=1)
    scaled = (gates_here[:, None] * slot_grads.astype(jnp.float32)).astype(jnp.bfloat16)
    grad_down = contract_rows(hidden, scaled).astype(jnp.bfloat16)
    part_hidden = contract_cols(scaled, down_weight)
    grad_hidden = lax.psum(part_hidden, "dp")
    gate_side, up_side = gated_grads(grad_hidden, pre_gate, pre_up, sigmoid_gate)
    gate_total = lax.psum(gate_part, "dp")
    grad_gate_weight = contract_rows(slot_inputs, gate_side).astype(jnp.bfloat16)
    grad_up_weight = contract_rows(slot_inputs, up_side).astype(jnp.bfloat16)
    slot_back = contract_cols(gate_side, gate_weight) + contract_cols(up_side, up_weight)
    for bit_number in range(GROUP.bit_length() - 1):
        gate_total = gate_total + partner(gate_total, "expert", bit_number)
    outgoing = (
        jnp.zeros((owner_count * bucket_size, feature_cols), jnp.float32)
        .at[bucket_flat]
        .set(slot_back)
    )
    incoming = lax.all_to_all(
        outgoing.reshape(owner_count, bucket_size, feature_cols),
        "expert",
        split_axis=0,
        concat_axis=0,
        tiled=True,
    )
    target = jnp.where(send_valid, send_index, token_rows)
    summed = (
        jnp.zeros((token_rows + 1, feature_cols), jnp.float32)
        .at[target.reshape(-1)]
        .add(incoming.reshape(-1, feature_cols))
    )
    grad_tokens = summed[:token_rows].astype(jnp.bfloat16)
    gate_width = capacity // GROUP
    grad_gates = lax.dynamic_slice_in_dim(gate_total, quarter * gate_width, gate_width)[None, :]
    return (grad_tokens, grad_gate_weight[None], grad_up_weight[None], grad_down[None], grad_gates)


def solution(mesh):
    in_specs = (
        P("expert", "dp"),
        P("expert", "dp"),
        P(),
        P(),
        P("expert", "dp", None),
        P("expert", "dp", None),
        P("expert", None, "dp"),
    )
    out_specs = (
        P("expert", "dp"),
        P("expert", "dp", None),
        P("expert", "dp", None),
        P("expert", None, "dp"),
        P("expert", None),
    )
    return jax.shard_map(
        per_device, mesh=mesh, in_specs=in_specs, out_specs=out_specs, check_vma=False
    )
```

profile of v0, /device:TPU:2, one launch (start us, length us, event | category | flops | bytes accessed | tf_op | source)
XLA Modules:
  0.0 412.5 jit_solution(8496324978233504566)
XLA Ops:
  7.2 0.0 copy-start
  7.2 0.8 broadcast_subtract_fusion
  7.9 0.1 reshape.203
  8.1 2.3 reduce-window.6
  10.3 0.1 slice.37
  10.4 0.1 copy.15
  10.6 0.1 bitcast_bitcast_fusion
  10.7 0.1 reshape.195
  10.8 29.9 %scatter_fusion = s32[4,21]{1,0:T(4,128)S(1)} fusion(s32[4,21]{1,0:T(4,128)S(1)} %broadcast.144.clone.1, s32[640]{0:T(1024)S(1)} %reshape.195, s32[640]{0:T(1024)S(1)} %broadcast.189), kind=kCustom, calls=%fused_computation.4 | custom fusion | bytes 12800 | tf_op jit(solution)/shard_map/scatter | solution.py:65
  40.7 0.0 copy-start.1
  40.7 29.9 %scatter_fusion.1 = s32[4,21]{1,0:T(4,128)S(1)} fusion(s32[4,21]{1,0:T(4,128)S(1)} %broadcast.144.clone, s32[640]{0:T(1024)S(1)} %reshape.195, s32[640]{0:T(1024)S(1)} %reshape.203), kind=kCustom, calls=%fused_computation.5 | custom fusion | bytes 12800 | tf_op jit(solution)/shard_map/scatter | solution.py:60
  70.6 0.0 copy-start.2
  70.6 0.1 reshape.165
  70.7 0.0 copy-done.1
  70.7 1.4 gather_fusion.2
  72.2 0.0 copy-done.2
  72.2 1.4 gather_fusion
  73.6 0.8 broadcast_select_fusion.1
  74.4 9.2 %all-to-all-start = ((bf16[16,20,128]{2,1,0:T(8,128)(2,1)}), bf16[16,20,128]{2,1,0:T(8,128)(2,1)S(1)}, u32[]{:S(2)}, u32[]{:S(2)}) async-start(bf16[16,20,128]{2,1,0:T(8,128)(2,1)} %get-tuple-element.13), calls=%async_computation | async-start | bytes 196608 | tf_op jit(solution)/shard_map/all_to_all | solution.py:73
  83.7 6.4 %all-to-all-done = bf16[16,20,128]{2,1,0:T(8,128)(2,1)S(1)} async-done(((bf16[16,20,128]{2,1,0:T(8,128)(2,1)}), bf16[16,20,128]{2,1,0:T(8,128)(2,1)S(1)}, u32[]{:S(2)}, u32[]{:S(2)}) %all-to-all-start) | async-done | bytes 81952 | tf_op jit(solution)/shard_map/all_to_all | solution.py:73
  90.0 5.0 %all-to-all-start.1 = ((bf16[16,20,128]{2,1,0:T(8,128)(2,1)}), bf16[16,20,128]{2,1,0:T(8,128)(2,1)S(1)}, u32[]{:S(2)}, u32[]{:S(2)}) async-start(bf16[16,20,128]{2,1,0:T(8,128)(2,1)} %get-tuple-element.14), calls=%async_computation.1 | async-start | bytes 196608 | tf_op jit(solution)/shard_map/all_to_all | solution.py:72
  95.0 0.0 all-reduce.4.cloned.1.call-start
  95.0 0.7 constant_dynamic-slice_fusion
  95.7 0.0 copy-start.4
  95.8 0.8 gather_fusion.1
  96.5 4.8 %all-to-all-done.1 = bf16[16,20,128]{2,1,0:T(8,128)(2,1)S(1)} async-done(((bf16[16,20,128]{2,1,0:T(8,128)(2,1)}), bf16[16,20,128]{2,1,0:T(8,128)(2,1)S(1)}, u32[]{:S(2)}, u32[]{:S(2)}) %all-to-all-start.1) | async-done | bytes 81952 | tf_op jit(solution)/shard_map/all_to_all | solution.py:72
  101.3 0.8 gather_fusion.3
  102.1 0.0 copy-done
  102.1 1.4 fusion.6
  103.5 0.0 copy-done.4
  103.5 0.0 copy-start.3
  103.5 1.4 fusion.9
  104.9 0.0 copy-done.3
  104.9 1.5 fusion.12
  106.4 0.0 all-reduce.4.cloned.1.call-update
  106.4 0.1 select_n.96
  106.5 221.0 %all-reduce.4.cloned.1.call-done = (f32[160,2048]{1,0:T(8,128)}, f32[160,2048]{1,0:T(8,128)}, f32[160,2048]{1,0:T(8,128)}) async-done(((f32[160,2048]{1,0:T(8,128)}, f32[160,2048]{1,0:T(8,128)}, f32[160,2048]{1,0:T(8,128)}), (f32[160,2048]{1,0:T(8,128)}, f32[160,2048]{1,0:T(8,128)}, f32[160,2048]{1,0:T(8,128)})) %all-reduce.4.cloned.1.call-update) | async-done | bytes 3932176 | tf_op jit(solution)/shard_map/psum | solution.py:88
  327.6 3.0 multiply_convert_fusion
  330.6 0.4 fusion.3
  331.0 1.3 fusion.2
  332.3 49.1 %psum.31 = f32[160]{0:T(256)S(1)} all-reduce(f32[160]{0:T(256)S(1)} %fusion.3), channel_id=1, replica_groups=mesh['dp'=32,'expert'=16] {'dp'}, use_global_device_ids=true, to_apply=%region_11.12 | all-reduce | flops 160 | bytes 1280 | tf_op jit(solution)/shard_map/psum | solution.py:98
  381.4 3.4 collective-permute-start
  384.8 0.4 fusion.4
  385.2 0.3 convolution_add_fusion
  385.5 1.1 fusion
  386.7 1.0 scatter_custom_fusion.2
  387.7 0.7 reshape.160
  388.3 7.0 %all-to-all-start.2 = ((f32[16,20,128]{2,1,0:T(8,128)}), f32[16,20,128]{2,1,0:T(8,128)S(1)}, u32[]{:S(2)}, u32[]{:S(2)}) async-start(f32[16,20,128]{2,1,0:T(8,128)} %reshape.160), calls=%async_computation.2 | async-start | bytes 393216 | tf_op jit(solution)/shard_map/all_to_all | solution.py:109
  395.3 0.0 collective-permute-done
  395.3 4.9 %collective-permute-start.1 = (f32[160]{0:T(256)S(1)}, f32[160]{0:T(256)S(1)}, u32[]{:S(2)}, u32[]{:S(2)}) collective-permute-start(f32[160]{0:T(256)S(1)} %add.108), channel_id=1, source_target_pairs={{0,2},{1,3},{2,0},{3,1},{4,6},{5,7},{6,4},{7,5},{8,10},{9,11},{10,... | collective-permute-start | bytes 1928 | tf_op jit(solution)/shard_map/ppermute | solution.py:12
  400.2 1.1 fusion.1
  401.3 1.0 collective-permute-done.1
  402.3 0.6 dynamic-slice_bitcast_fusion
  402.9 0.0 all-to-all-done.2
  402.9 2.0 scatter_custom_fusion.3
  405.0 0.6 slice.48
  (26 shorter events, 0.3 us)
Async XLA Ops:
  7.2 94.9 %copy-start = (bf16[1,128,2048]{2,1,0:T(8,128)(2,1)S(1)}, bf16[1,128,2048]{2,1,0:T(8,128)(2,1)}, u32[]{:S(2)}) copy-start(bf16[1,128,2048]{2,1,0:T(8,128)(2,1)} %param.11) | copy-start | bytes 1572868
  40.7 30.0 %copy-start.1 = (bf16[320,128]{1,0:T(8,128)(2,1)S(1)}, bf16[320,128]{1,0:T(8,128)(2,1)}, u32[]{:S(2)}) copy-start(bf16[320,128]{1,0:T(8,128)(2,1)} %param.7) | copy-start | bytes 245764
  70.6 1.6 copy-start.2
  74.4 15.6 %all-to-all-start = ((bf16[16,20,128]{2,1,0:T(8,128)(2,1)}), bf16[16,20,128]{2,1,0:T(8,128)(2,1)S(1)}, u32[]{:S(2)}, u32[]{:S(2)}) async-start(bf16[16,20,128]{2,1,0:T(8,128)(2,1)} %get-tuple-element.13), calls=%async_computation | async-start | bytes 196608 | tf_op jit(solution)/shard_map/all_to_all | solution.py:73
  90.0 11.3 %all-to-all-start.1 = ((bf16[16,20,128]{2,1,0:T(8,128)(2,1)}), bf16[16,20,128]{2,1,0:T(8,128)(2,1)S(1)}, u32[]{:S(2)}, u32[]{:S(2)}) async-start(bf16[16,20,128]{2,1,0:T(8,128)(2,1)} %get-tuple-element.14), calls=%async_computation.1 | async-start | bytes 196608 | tf_op jit(solution)/shard_map/all_to_all | solution.py:72
  95.0 232.6 %all-reduce.4.cloned.1.call-start = ((), (), s32[]{:S(2)}) async-start(), calls=%async_computation.3 | async-start | bytes 7864320 | tf_op jit(solution)/shard_map/psum | solution.py:88
  95.7 7.8 %copy-start.4 = (bf16[1,128,2048]{2,1,0:T(8,128)(2,1)S(1)}, bf16[1,128,2048]{2,1,0:T(8,128)(2,1)}, u32[]{:S(2)}) copy-start(bf16[1,128,2048]{2,1,0:T(8,128)(2,1)} %param.12) | copy-start | bytes 1572868
  103.5 1.4 copy-start.3
  381.4 13.9 %collective-permute-start = (f32[160]{0:T(256)S(1)}, f32[160]{0:T(256)S(1)}, u32[]{:S(2)}, u32[]{:S(2)}) collective-permute-start(f32[160]{0:T(256)S(1)} %psum.31), channel_id=1, source_target_pairs={{0,1},{1,0},{2,3},{3,2},{4,5},{5,4},{6,7},{7,6},{8,9},{9,8},{10,11... | collective-permute-start | bytes 1928 | tf_op jit(solution)/shard_map/ppermute | solution.py:12
  388.3 14.6 %all-to-all-start.2 = ((f32[16,20,128]{2,1,0:T(8,128)}), f32[16,20,128]{2,1,0:T(8,128)S(1)}, u32[]{:S(2)}, u32[]{:S(2)}) async-start(f32[16,20,128]{2,1,0:T(8,128)} %reshape.160), calls=%async_computation.2 | async-start | bytes 393216 | tf_op jit(solution)/shard_map/all_to_all | solution.py:109
  395.3 7.0 %collective-permute-start.1 = (f32[160]{0:T(256)S(1)}, f32[160]{0:T(256)S(1)}, u32[]{:S(2)}, u32[]{:S(2)}) collective-permute-start(f32[160]{0:T(256)S(1)} %add.108), channel_id=1, source_target_pairs={{0,2},{1,3},{2,0},{3,1},{4,6},{5,7},{6,4},{7,5},{8,10},{9,11},{10,... | collective-permute-start | bytes 1928 | tf_op jit(solution)/shard_map/ppermute | solution.py:12
Sparse Core Ops, SparseCore 0:
  106.5 221.0 all-reduce.3
where the time goes:
time: 413 us; the launch traced here: 412 us
  waiting for transfers between devices  233 us (56%)
  local copies, waits for them, and re-layouts  68.4 us (17%)
  blocking collectives  49.1 us (12%)
  starting transfers between devices  29.4 us (7%)
  between operations  14.3 us (3%)
  other arithmetic  9.07 us (2%)
  matrix products  8.98 us (2%)
    psum x1, waiting for transfers between devices, per_device(): pre_gate, pre_up = lax.psum((part_gate, part_up), 'dp')  221 us
    psum x1, blocking collectives, per_device(): gate_total = lax.psum(gate_part, 'dp')  49.1 us
    scatter x1, local copies, waits for them, and re-layouts, per_device(): send_table = jnp.zeros((flight_count, bucket_size + 1), jnp.int32).at[exp...  29.9 us
    scatter x1, local copies, waits for them, and re-layouts, per_device(): filled = jnp.zeros((flight_count, bucket_size + 1), jnp.int32).at[expert_...  29.9 us
    all_to_all x1, starting transfers between devices, per_device(): lax.all_to_all(grad_send, 'expert', split_axis=0, concat_axis=0, tiled=True)  9.2 us
    ppermute x2, starting transfers between devices, partner(): return lax.ppermute(value, axis, pairs)  8.27 us
  transfers between devices with their start and end apart: 6, of which 4 were waited for; matrix products, arithmetic and copies ran while one was open for 2% of the time, Pallas kernels for 0%

commit v1 on v0

--- a/solution.py
+++ b/solution.py
@@ -95,7 +95,7 @@
     part_hidden = contract_cols(scaled, down_weight)
     grad_hidden = lax.psum(part_hidden, "dp")
     gate_side, up_side = gated_grads(grad_hidden, pre_gate, pre_up, sigmoid_gate)
-    gate_total = lax.psum(gate_part, "dp")
+    gate_total = jnp.sum(lax.all_gather(gate_part, "dp"), axis=0)
     grad_gate_weight = contract_rows(slot_inputs, gate_side).astype(jnp.bfloat16)
     grad_up_weight = contract_rows(slot_inputs, up_side).astype(jnp.bfloat16)
     slot_back = contract_cols(gate_side, gate_weight) + contract_cols(up_side, up_weight)

time: 413 us -> 458 us (1.11)
  blocking collectives: 49.1 us -> 93.3 us
    unnamed x0 -> x1, blocking collectives: none -> 93.3 us
    psum x1 -> x0, blocking collectives: 49.1 us -> none  [per_device(): gate_total = lax.psum(gate_part, 'dp')]
where the time goes in v1:
time: 458 us; the launch traced here: 457 us
  waiting for transfers between devices  231 us (50%)
  blocking collectives  93.3 us (20%)
  local copies, waits for them, and re-layouts  70 us (15%)
  starting transfers between devices  29.4 us (6%)
  between operations  15 us (3%)
  other arithmetic  9.13 us (2%)
  matrix products  8.95 us (2%)
    psum x1, waiting for transfers between devices, per_device(): pre_gate, pre_up = lax.psum((part_gate, part_up), 'dp')  219 us
    unnamed x1, blocking collectives  93.3 us
    scatter x1, local copies, waits for them, and re-layouts, per_device(): filled = jnp.zeros((flight_count, bucket_size + 1), jnp.int32).at[expert_...  29.9 us
    scatter x1, local copies, waits for them, and re-layouts, per_device(): send_table = jnp.zeros((flight_count, bucket_size + 1), jnp.int32).at[exp...  29.9 us
    all_to_all x1, starting transfers between devices, per_device(): lax.all_to_all(input_send, 'expert', split_axis=0, concat_axis=0, tiled=T...  9.2 us
  transfers between devices with their start and end apart: 6, of which 4 were waited for; matrix products, arithmetic and copies ran while one was open for 2% of the time, Pallas kernels for 0%

profile of v1, /device:TPU:2, one launch (start us, length us, event | category | flops | bytes accessed | tf_op | source)
XLA Modules:
  0.0 457.1 jit_solution(13081997900001145920)
XLA Ops:
  7.2 0.0 copy-start
  7.2 0.8 broadcast_subtract_fusion
  8.0 2.3 reduce-window.6
  10.3 0.1 slice.37
  10.3 0.1 copy.19
  10.5 0.1 bitcast_bitcast_fusion
  10.6 0.1 reshape.195
  10.7 0.1 reshape.203
  10.8 29.9 %scatter_fusion = s32[4,21]{1,0:T(4,128)S(1)} fusion(s32[4,21]{1,0:T(4,128)S(1)} %broadcast.144.clone.1, s32[640]{0:T(1024)S(1)} %reshape.195, s32[640]{0:T(1024)S(1)} %broadcast.189), kind=kCustom, calls=%fused_computation.4 | custom fusion | bytes 12800 | tf_op jit(solution)/shard_map/scatter | solution.py:65
  40.7 0.0 copy-start.1
  40.7 29.9 %scatter_fusion.1 = s32[4,21]{1,0:T(4,128)S(1)} fusion(s32[4,21]{1,0:T(4,128)S(1)} %broadcast.144.clone, s32[640]{0:T(1024)S(1)} %reshape.195, s32[640]{0:T(1024)S(1)} %reshape.203), kind=kCustom, calls=%fused_computation.5 | custom fusion | bytes 12800 | tf_op jit(solution)/shard_map/scatter | solution.py:60
  70.6 0.0 copy-start.2
  70.6 0.1 reshape.165
  70.7 0.0 copy-done.1
  70.7 1.4 gather_fusion
  72.2 0.0 copy-done.2
  72.2 1.4 gather_fusion.2
  73.7 0.8 broadcast_select_fusion.1
  74.4 9.2 %all-to-all-start.1 = ((bf16[16,20,128]{2,1,0:T(8,128)(2,1)}), bf16[16,20,128]{2,1,0:T(8,128)(2,1)S(1)}, u32[]{:S(2)}, u32[]{:S(2)}) async-start(bf16[16,20,128]{2,1,0:T(8,128)(2,1)} %get-tuple-element.14), calls=%async_computation.1 | async-start | bytes 196608 | tf_op jit(solution)/shard_map/all_to_all | solution.py:72
  83.7 6.4 %all-to-all-done.1 = bf16[16,20,128]{2,1,0:T(8,128)(2,1)S(1)} async-done(((bf16[16,20,128]{2,1,0:T(8,128)(2,1)}), bf16[16,20,128]{2,1,0:T(8,128)(2,1)S(1)}, u32[]{:S(2)}, u32[]{:S(2)}) %all-to-all-start.1) | async-done | bytes 81952 | tf_op jit(solution)/shard_map/all_to_all | solution.py:72
  90.0 5.0 %all-to-all-start = ((bf16[16,20,128]{2,1,0:T(8,128)(2,1)}), bf16[16,20,128]{2,1,0:T(8,128)(2,1)S(1)}, u32[]{:S(2)}, u32[]{:S(2)}) async-start(bf16[16,20,128]{2,1,0:T(8,128)(2,1)} %get-tuple-element.13), calls=%async_computation | async-start | bytes 196608 | tf_op jit(solution)/shard_map/all_to_all | solution.py:73
  95.0 0.0 all-reduce.5.cloned.1.call-start
  95.0 0.7 constant_dynamic-slice_fusion
  95.8 0.0 copy-start.4
  95.8 0.8 gather_fusion.3
  96.5 4.8 %all-to-all-done = bf16[16,20,128]{2,1,0:T(8,128)(2,1)S(1)} async-done(((bf16[16,20,128]{2,1,0:T(8,128)(2,1)}), bf16[16,20,128]{2,1,0:T(8,128)(2,1)S(1)}, u32[]{:S(2)}, u32[]{:S(2)}) %all-to-all-start) | async-done | bytes 81952 | tf_op jit(solution)/shard_map/all_to_all | solution.py:73
  101.3 0.8 gather_fusion.1
  102.1 0.0 copy-done
  102.1 1.4 fusion.6
  103.5 0.0 copy-done.4
  103.5 0.0 copy-start.3
  103.5 1.4 fusion.9
  104.9 0.0 copy-done.3
  104.9 1.5 fusion.12
  106.4 0.0 all-reduce.5.cloned.1.call-update
  106.4 0.1 select_n.96
  106.5 1.3 dynamic-slice
  108.5 219.1 %all-reduce.5.cloned.1.call-done = (f32[160,2048]{1,0:T(8,128)}, f32[160,2048]{1,0:T(8,128)}, f32[160,2048]{1,0:T(8,128)}) async-done(((f32[160,2048]{1,0:T(8,128)}, f32[160,2048]{1,0:T(8,128)}, f32[160,2048]{1,0:T(8,128)}), (f32[160,2048]{1,0:T(8,128)}, f32[160,2048]{1,0:T(8,128)}, f32[160,2048]{1,0:T(8,128)})) %all-reduce.5.cloned.1.call-update) | async-done | bytes 3932176 | tf_op jit(solution)/shard_map/psum | solution.py:88
  327.6 3.0 multiply_convert_fusion
  330.6 1.3 fusion.2
  331.9 0.4 fusion.3
  332.4 0.4 fusion.4
  332.8 0.3 dynamic-update-slice
  333.1 93.3 %all-reduce.1 = f32[5120]{0:T(1024)S(1)} all-reduce(f32[5120]{0:T(1024)S(1)} %dynamic-update-slice), channel_id=2, replica_groups=mesh['dp'=32,'expert'=16] {'dp'}, use_global_device_ids=true, to_apply=%add.1 | all-reduce | flops 5120 | bytes 40960
  426.3 0.1 reshape.223
  426.4 3.4 collective-permute-start
  429.8 0.3 convolution_add_fusion
  430.2 1.1 fusion
  431.3 1.0 scatter_custom_fusion.2
  432.3 0.7 reshape.160
  433.0 7.0 %all-to-all-start.2 = ((f32[16,20,128]{2,1,0:T(8,128)}), f32[16,20,128]{2,1,0:T(8,128)S(1)}, u32[]{:S(2)}, u32[]{:S(2)}) async-start(f32[16,20,128]{2,1,0:T(8,128)} %reshape.160), calls=%async_computation.2 | async-start | bytes 393216 | tf_op jit(solution)/shard_map/all_to_all | solution.py:109
  440.0 0.0 collective-permute-done
  440.0 4.9 %collective-permute-start.1 = (f32[160]{0:T(256)S(1)}, f32[160]{0:T(256)S(1)}, u32[]{:S(2)}, u32[]{:S(2)}) collective-permute-start(f32[160]{0:T(256)S(1)} %add.106), channel_id=1, source_target_pairs={{0,2},{1,3},{2,0},{3,1},{4,6},{5,7},{6,4},{7,5},{8,10},{9,11},{10,... | collective-permute-start | bytes 1928 | tf_op jit(solution)/shard_map/ppermute | solution.py:12
  444.9 1.1 fusion.1
  446.0 1.0 collective-permute-done.1
  447.0 0.6 dynamic-slice_bitcast_fusion
  447.6 0.0 all-to-all-done.2
  447.6 2.0 scatter_custom_fusion.3
  449.6 0.6 slice.48
  (28 shorter events, 0.3 us)
Async XLA Ops:
  7.2 94.9 %copy-start = (bf16[1,128,2048]{2,1,0:T(8,128)(2,1)S(1)}, bf16[1,128,2048]{2,1,0:T(8,128)(2,1)}, u32[]{:S(2)}) copy-start(bf16[1,128,2048]{2,1,0:T(8,128)(2,1)} %param.11) | copy-start | bytes 1572868
  40.7 30.0 %copy-start.1 = (bf16[320,128]{1,0:T(8,128)(2,1)S(1)}, bf16[320,128]{1,0:T(8,128)(2,1)}, u32[]{:S(2)}) copy-start(bf16[320,128]{1,0:T(8,128)(2,1)} %param.8) | copy-start | bytes 245764
  70.6 1.6 copy-start.2
  74.4 15.6 %all-to-all-start.1 = ((bf16[16,20,128]{2,1,0:T(8,128)(2,1)}), bf16[16,20,128]{2,1,0:T(8,128)(2,1)S(1)}, u32[]{:S(2)}, u32[]{:S(2)}) async-start(bf16[16,20,128]{2,1,0:T(8,128)(2,1)} %get-tuple-element.14), calls=%async_computation.1 | async-start | bytes 196608 | tf_op jit(solution)/shard_map/all_to_all | solution.py:72
  90.0 11.3 %all-to-all-start = ((bf16[16,20,128]{2,1,0:T(8,128)(2,1)}), bf16[16,20,128]{2,1,0:T(8,128)(2,1)S(1)}, u32[]{:S(2)}, u32[]{:S(2)}) async-start(bf16[16,20,128]{2,1,0:T(8,128)(2,1)} %get-tuple-element.13), calls=%async_computation | async-start | bytes 196608 | tf_op jit(solution)/shard_map/all_to_all | solution.py:73
  95.0 232.6 %all-reduce.5.cloned.1.call-start = ((), (), s32[]{:S(2)}) async-start(), calls=%async_computation.3 | async-start | bytes 7864320 | tf_op jit(solution)/shard_map/psum | solution.py:88
  95.8 7.8 %copy-start.4 = (bf16[1,128,2048]{2,1,0:T(8,128)(2,1)S(1)}, bf16[1,128,2048]{2,1,0:T(8,128)(2,1)}, u32[]{:S(2)}) copy-start(bf16[1,128,2048]{2,1,0:T(8,128)(2,1)} %param.12) | copy-start | bytes 1572868
  103.5 1.4 copy-start.3
  426.4 13.5 %collective-permute-start = (f32[160]{0:T(256)S(1)}, f32[160]{0:T(256)S(1)}, u32[]{:S(2)}, u32[]{:S(2)}) collective-permute-start(f32[160]{0:T(256)S(1)} %reduce_sum.29), channel_id=1, source_target_pairs={{0,1},{1,0},{2,3},{3,2},{4,5},{5,4},{6,7},{7,6},{8,9},{9,8},{10,11... | collective-permute-start | bytes 1928 | tf_op jit(solution)/shard_map/ppermute | solution.py:12
  433.0 14.6 %all-to-all-start.2 = ((f32[16,20,128]{2,1,0:T(8,128)}), f32[16,20,128]{2,1,0:T(8,128)S(1)}, u32[]{:S(2)}, u32[]{:S(2)}) async-start(f32[16,20,128]{2,1,0:T(8,128)} %reshape.160), calls=%async_computation.2 | async-start | bytes 393216 | tf_op jit(solution)/shard_map/all_to_all | solution.py:109
  440.0 7.0 %collective-permute-start.1 = (f32[160]{0:T(256)S(1)}, f32[160]{0:T(256)S(1)}, u32[]{:S(2)}, u32[]{:S(2)}) collective-permute-start(f32[160]{0:T(256)S(1)} %add.106), channel_id=1, source_target_pairs={{0,2},{1,3},{2,0},{3,1},{4,6},{5,7},{6,4},{7,5},{8,10},{9,11},{10,... | collective-permute-start | bytes 1928 | tf_op jit(solution)/shard_map/ppermute | solution.py:12
Sparse Core Ops, SparseCore 0:
  106.5 221.0 all-reduce.4
